TPU v7x, 256 devices: a whole 4x4x8 slice. The times are simulated.
256 devices in a mesh: row: 32 (over y, z), col: 8 (over x, core).
Axes of the slice: x: 4, y: 4, z: 8, core: 2. Of those that a mesh axis runs over, the one named last changes fastest.
Arguments:
- points: float32 [65536, 16], P(('row', 'col')), may hold values from -6 to 6
- inv_lengths: float32 [16], replicated, may hold values from 0.35 to 0.7
- signal_level: float32 [1], replicated, may hold values from 0.5 to 2
- noise_level: float32 [1], replicated, may hold values from 0.05 to 0.5
- right_sides: float32 [65536, 32], P(('row', 'col')), may hold values from -6 to 6
- block_counts: int32 [256], P(('row', 'col')), may hold values from 1 to 256, 49152 in all
Outputs:
- solution: float32 [65536, 32], P(('row', 'col'))
- residual: float32 [65536, 32], P(('row', 'col'))
Inputs may be any that keep to these rules, and one draw needn't show every extreme that they name: `block_counts`: each block of 256 slots holds its valid points first; the slots after them are padding.
All inputs are finite; a program needn't handle non-finite values.
Results may differ from a plain program's by a relative error of at most 0.012.
The roundings to bfloat16 on the way count: a program that leaves them out, or rounds other values in their place, can miss the bound.
Values may be sent and summed in bfloat16 or wider, within the bound.
A program may use at most 64 MiB of HBM per device.

v0:
```python
import math
import jax
import jax.numpy as jnp
from jax import lax
from jax.sharding import PartitionSpec as P

ITERS = 2


def kernel_tile(scaled_rows, square_rows, scaled_cols, square_cols, signal):
    inner_product = lax.dot_general(
        scaled_rows,
        scaled_cols,
        (((1,), (1,)), ((), ())),
        precision=lax.Precision.HIGHEST,
        preferred_element_type=jnp.float32,
    )
    distance = square_rows[:, None] + square_cols[None, :] - 2.0 * inner_product
    return (signal * jnp.exp(-0.5 * distance)).astype(jnp.bfloat16)


def column_norm(residual):
    return lax.psum(jnp.sum(residual * residual, axis=0), ("row", "col"))


def column_sweep(scaled_rows, square_rows, scaled_cols, square_cols, direction, signal):
    feat_count = scaled_rows.shape[1]
    zero_rows = jnp.zeros((scaled_rows.shape[0], direction.shape[1]), jnp.float32)
    running = zero_rows
    piece = lax.all_gather(direction, "row", axis=0, tiled=True)
    piece_rows = piece.shape[0]
    sub_rows = math.gcd(piece_rows, 512)
    pieces_count = piece_rows // sub_rows

    def advance(carried, parts):
        scaled_part, square_part, dir_part = parts
        kernel_block = kernel_tile(scaled_rows, square_rows, scaled_part, square_part, signal)
        return (carried + jnp.dot(kernel_block, dir_part, preferred_element_type=jnp.float32), None)

    running, unused = lax.scan(
        advance,
        running,
        (
            scaled_cols.reshape(pieces_count, sub_rows, feat_count),
            square_cols.reshape(pieces_count, sub_rows),
            piece.reshape(pieces_count, sub_rows, piece.shape[1]),
        ),
    )
    return running


def body(points, inv_lengths, signal_level, noise_level, right_sides, block_counts):
    block_rows = points.shape[0]
    signal = signal_level[0]
    noise_var = noise_level[0]
    scaled_own = points * inv_lengths[None, :]
    scaled_rows = lax.all_gather(scaled_own, "col", axis=0, tiled=True)
    square_rows = jnp.sum(scaled_rows * scaled_rows, axis=1)
    scaled_cols = lax.all_gather(scaled_own, "row", axis=0, tiled=True)
    square_cols = jnp.sum(scaled_cols * scaled_cols, axis=1)
    slots = jnp.arange(block_rows, dtype=jnp.int32)
    valid_rows = (slots < block_counts[0]).astype(jnp.float32)[:, None]
    residual = valid_rows * right_sides
    solution = jnp.zeros_like(residual)
    direction = residual.astype(jnp.bfloat16)
    norm_now = column_norm(residual)
    for iteration in range(ITERS):
        dir_float = direction.astype(jnp.float32)
        forward = column_sweep(
            scaled_rows, square_rows, scaled_cols, square_cols, direction, signal
        )
        reduced = lax.psum_scatter(forward, "col", scatter_dimension=0, tiled=True)
        applied = valid_rows * reduced + noise_var * dir_float
        curvature = lax.psum(jnp.sum(dir_float * applied, axis=0), ("row", "col"))
        applied, curvature = (applied, curvature)
        dir_float = direction.astype(jnp.float32)
        step_size = norm_now / curvature
        solution = solution + step_size * dir_float
        residual = residual - step_size * applied
        if iteration + 1 < ITERS:
            norm_next = column_norm(residual)
            direction = (residual + norm_next / norm_now * dir_float).astype(jnp.bfloat16)
            norm_now = norm_next
    return (solution, residual)


def solution(mesh):
    in_specs = (P(("row", "col"), None), P(), P(), P(), P(("row", "col"), None), P(("row", "col")))
    out_specs = (P(("row", "col"), None), P(("row", "col"), None))
    return jax.shard_map(body, mesh=mesh, in_specs=in_specs, out_specs=out_specs, check_vma=False)
```

profile of v0, /device:TPU:1, one launch (start us, length us, event | category | flops | bytes accessed | tf_op | source)
XLA Modules:
  0.0 683.2 jit_solution(8978833498880750130)
XLA Ops:
  8.0 15.8 %all_gather.12 = f32[2048,16]{0,1:T(8,128)S(1)} all-gather(f32[256,16]{0,1:T(8,128)S(1)} %broadcast_multiply_fusion), channel_id=1, replica_groups=mesh['row'=32,'col'=8] {'col'}, dimensions={0}, use_global_device_ids=true | all-gather | bytes 147456 | tf_op jit(solution)/shard_map/all_gather | solution.py:57
  23.8 39.8 %all_gather.13 = f32[8192,16]{0,1:T(8,128)S(1)} all-gather(f32[256,16]{0,1:T(8,128)S(1)} %broadcast_multiply_fusion), channel_id=1, replica_groups=mesh['row'=32,'col'=8] {'row'}, dimensions={0}, use_global_device_ids=true | all-gather | bytes 540672 | tf_op jit(solution)/shard_map/all_gather | solution.py:59
  65.0 32.2 %all_gather.14 = bf16[8192,32]{0,1:T(8,128)(2,1)S(1)} all-gather(bf16[256,32]{0,1:T(8,128)(2,1)S(1)} %multiply_convert_fusion), channel_id=1, replica_groups=mesh['row'=32,'col'=8] {'row'}, dimensions={0}, use_global_device_ids=true | all-gather | bytes 540672 | tf_op jit(solution)/shard_map/all_gather | solution.py:30
  99.3 109.9 %while.22 = (s32[]{:T(128)}, f32[2048,32]{0,1:T(8,128)S(1)}, f32[]{:T(128)}, f32[2048]{0:T(1024)S(1)}, f32[16,512]{1,0:T(8,128)S(1)}, /*index=5*/f32[16,512,16]{...) while((s32[]{:T(128)}, f32[2048,32]{0,1:T(8,128)S(1)}, ...), condition=%wide.region_5.6_spmd.clone, body=%wide.region_4.5_spmd.clone.sunk | while | flops 274857984 | bytes 5028475 | solution.py:40
  106.2 5.2 fusion.45
  113.0 5.2 fusion.45
  119.9 5.2 fusion.45
  126.8 5.2 fusion.45
  133.6 5.2 fusion.45
  210.6 48.9 %reduce-scatter.3.cloned.1.call-done = f32[256,32]{0,1:T(8,128)} async-done(((f32[2048,32]{0,1:T(8,128)}), f32[256,32]{0,1:T(8,128)}) %reduce-scatter.3.cloned.1.call-update) | async-done | bytes 32784 | tf_op jit(solution)/shard_map/reduce_scatter | solution.py:72
  260.4 78.2 %all-reduce = (f32[32]{0:T(128)S(1)}, f32[32]{0:T(128)S(1)}) all-reduce(f32[32]{0:T(128)S(1)} %get-tuple-element.175, f32[32]{0:T(128)S(1)} %get-tuple-element.174), channel_id=1, replica_groups=mesh['row'=32,'col'=8] {'row','col'}, use_global_device_ids=true, to_apply=%region_1.0 | all-reduce | flops 64 | bytes 512 | tf_op jit(solution)/shard_map/psum | solution.py:23
  339.6 73.1 %psum.30 = f32[32]{0:T(128)S(1)} all-reduce(f32[32]{0:T(128)S(1)} %get-tuple-element.210), channel_id=1, replica_groups=mesh['row'=32,'col'=8] {'row','col'}, use_global_device_ids=true, to_apply=%region_10.11 | all-reduce | flops 32 | bytes 256 | tf_op jit(solution)/shard_map/psum | solution.py:23
  412.7 33.5 %all_gather.15 = bf16[8192,32]{0,1:T(8,128)(2,1)S(1)} all-gather(bf16[256,32]{0,1:T(8,128)(2,1)S(1)} %fusion.26), channel_id=1, replica_groups=mesh['row'=32,'col'=8] {'row'}, dimensions={0}, use_global_device_ids=true | all-gather | bytes 540672 | tf_op jit(solution)/shard_map/all_gather | solution.py:30
  448.0 110.0 %while.23 = (s32[]{:T(128)}, f32[2048,32]{0,1:T(8,128)S(1)}, f32[]{:T(128)}, f32[2048]{0:T(1024)S(1)}, f32[16,512]{1,0:T(8,128)S(1)}, /*index=5*/f32[16,512,16]{...) while((s32[]{:T(128)}, f32[2048,32]{0,1:T(8,128)S(1)}, ...), condition=%wide.region_12.13_spmd.clone, body=%wide.region_11.12_spmd.clone.sunk | while | flops 274857984 | bytes 5028475 | solution.py:40
  448.0 5.2 fusion.50
  454.9 5.2 fusion.50
  461.8 5.2 fusion.50
  468.7 5.2 fusion.50
  475.5 5.2 fusion.50
  482.4 5.2 fusion.50
  489.3 5.2 fusion.50
  496.2 5.2 fusion.50
  503.0 5.2 fusion.50
  509.9 5.2 fusion.50
  516.8 5.2 fusion.50
  523.7 5.2 fusion.50
  530.5 5.2 fusion.50
  537.4 5.2 fusion.50
  544.3 5.2 fusion.50
  551.2 5.2 fusion.50
  558.7 37.0 %reduce-scatter.5.cloned.1.call-done = f32[256,32]{0,1:T(8,128)} async-done(((f32[2048,32]{0,1:T(8,128)}), f32[256,32]{0,1:T(8,128)}) %reduce-scatter.5.cloned.1.call-update) | async-done | bytes 32784 | tf_op jit(solution)/shard_map/reduce_scatter | solution.py:72
  596.6 78.2 %psum.31 = f32[32]{0:T(128)S(1)} all-reduce(f32[32]{0:T(128)S(1)} %fusion.21), channel_id=1, replica_groups=mesh['row'=32,'col'=8] {'row','col'}, use_global_device_ids=true, to_apply=%region_15.16 | all-reduce | flops 32 | bytes 256 | tf_op jit(solution)/shard_map/psum | solution.py:74
  (104 shorter events, 120.5 us)
Async XLA Ops:
  7.2 252.3 %reduce-scatter.3.cloned.1.call-start = ((), (), s32[]{:S(2)}) async-start(), calls=%async_computation.2 | async-start | bytes 294912 | tf_op jit(solution)/shard_map/reduce_scatter | solution.py:72
  99.2 160.3 %copy-start.2 = (f32[256,32]{0,1:T(8,128)S(1)}, f32[256,32]{0,1:T(8,128)}, u32[]{:S(2)}) copy-start(f32[256,32]{0,1:T(8,128)} %param.14) | copy-start | bytes 98308
  209.2 0.7 copy-start.1
  209.9 385.8 %reduce-scatter.5.cloned.1.call-start = ((), (), s32[]{:S(2)}) async-start(), calls=%async_computation.3 | async-start | bytes 294912 | tf_op jit(solution)/shard_map/reduce_scatter | solution.py:72
  558.0 0.7 copy-start
Sparse Core Ops, SparseCore 0:
  210.0 49.4 reduce-scatter.2
  558.8 36.8 reduce-scatter.4
where the time goes:
time: 685 us; the launch traced here: 683 us
  blocking collectives  351 us (51%)
  matrix products  218 us (32%)
  waiting for transfers between devices  85.9 us (13%)
  between operations  15.4 us (2%)
    dot_general x32, matrix products, kernel_tile(): lax.dot_general(scaled_rows, scaled_cols, (((1,), (1,)), ((), ())), preci...  166 us
    psum x2, blocking collectives, column_norm(): return lax.psum(jnp.sum(residual * residual, axis=0), ('row', 'col'))  151 us
    reduce_scatter x2, waiting for transfers between devices, body(): reduced = lax.psum_scatter(forward, 'col', scatter_dimension=0, tiled=True)  85.9 us
    psum x1, blocking collectives, body(): curvature = lax.psum(jnp.sum(dir_float * applied, axis=0), ('row', 'col'))  78.2 us
    all_gather x2, blocking collectives, column_sweep(): piece = lax.all_gather(direction, 'row', axis=0, tiled=True)  65.7 us
    dot_general x32, matrix products, advance(): jnp.dot(kernel_block, dir_part, preferred_element_type=jnp.float32)  52.1 us
    all_gather x1, blocking collectives, body(): scaled_cols = lax.all_gather(scaled_own, 'row', axis=0, tiled=True)  39.8 us
    all_gather x1, blocking collectives, body(): scaled_rows = lax.all_gather(scaled_own, 'col', axis=0, tiled=True)  15.8 us
  transfers between devices with their start and end apart: 2, of which 2 were waited for; matrix products, arithmetic and copies ran while one was open for 0% of the time, Pallas kernels for 0%

commit v1 on v0

--- a/solution.py
+++ b/solution.py
@@ -56,7 +56,9 @@
     scaled_own = points * inv_lengths[None, :]
     scaled_rows = lax.all_gather(scaled_own, "col", axis=0, tiled=True)
     square_rows = jnp.sum(scaled_rows * scaled_rows, axis=1)
-    scaled_cols = lax.all_gather(scaled_own, "row", axis=0, tiled=True)
+    scaled_cols = jnp.concatenate(
+        lax.all_to_all(jnp.stack([scaled_own] * lax.axis_size("row")), "row", 0, 0), axis=0
+    )
     square_cols = jnp.sum(scaled_cols * scaled_cols, axis=1)
     slots = jnp.arange(block_rows, dtype=jnp.int32)
     valid_rows = (slots < block_counts[0]).astype(jnp.float32)[:, None]

time: 685 us -> 649 us (0.947)
  blocking collectives: 351 us -> 325 us
  waiting for transfers between devices: 85.9 us -> 66.3 us
  starting transfers between devices: 0.08 us -> 12.1 us
    all_gather x1 -> x0, blocking collectives: 39.8 us -> none  [body(): scaled_cols = lax.all_gather(scaled_own, 'row', axis=0, tiled=True)]
    reduce_scatter x2, waiting for transfers between devices: 85.9 us -> 66.3 us  [body(): reduced = lax.psum_scatter(forward, 'col', scatter_dimension=0, tiled=True)]
    all_to_all x0 -> x1, starting transfers between devices: none -> 12 us  [body(): lax.all_to_all(jnp.stack([scaled_own] * lax.axis_size('row')), 'row', 0, 0)]
    all_gather x2, blocking collectives: 65.7 us -> 72.9 us  [column_sweep(): piece = lax.all_gather(direction, 'row', axis=0, tiled=True)]
    dot_general x32, matrix products: 52.1 us -> 45.1 us  [advance(): jnp.dot(kernel_block, dir_part, preferred_element_type=jnp.float32)]
  transfers between devices with their start and end apart: 2 -> 3, of which waited for: 2 -> 2; matrix products, arithmetic and copies ran while one was open for 0% -> 0% of each run, Pallas kernels for 0% -> 0%
where the time goes in v1:
time: 649 us; the launch traced here: 647 us
  blocking collectives  325 us (50%)
  matrix products  214 us (33%)
  waiting for transfers between devices  66.3 us (10%)
  between operations  15.5 us (2%)
  starting transfers between devices  12.1 us (2%)
  local copies, waits for them, and re-layouts  6.9 us (1%)
    dot_general x32, matrix products, kernel_tile(): lax.dot_general(scaled_rows, scaled_cols, (((1,), (1,)), ((), ())), preci...  169 us
    psum x2, blocking collectives, column_norm(): return lax.psum(jnp.sum(residual * residual, axis=0), ('row', 'col'))  151 us
    psum x1, blocking collectives, body(): curvature = lax.psum(jnp.sum(dir_float * applied, axis=0), ('row', 'col'))  78.2 us
    all_gather x2, blocking collectives, column_sweep(): piece = lax.all_gather(direction, 'row', axis=0, tiled=True)  72.9 us
    reduce_scatter x2, waiting for transfers between devices, body(): reduced = lax.psum_scatter(forward, 'col', scatter_dimension=0, tiled=True)  66.3 us
    dot_general x32, matrix products, advance(): jnp.dot(kernel_block, dir_part, preferred_element_type=jnp.float32)  45.1 us
    all_gather x1, blocking collectives, body(): scaled_rows = lax.all_gather(scaled_own, 'col', axis=0, tiled=True)  22.6 us
  transfers between devices with their start and end apart: 3, of which 2 were waited for; matrix products, arithmetic and copies ran while one was open for 0% of the time, Pallas kernels for 0%

profile of v1, /device:TPU:1, one launch (start us, length us, event | category | flops | bytes accessed | tf_op | source)
XLA Modules:
  0.0 646.8 jit_solution(5350321345478631937)
XLA Ops:
  8.8 12.0 %all-to-all-start = ((f32[32,256,16]{1,2,0:T(8,128)}), f32[32,256,16]{1,2,0:T(8,128)S(1)}, u32[]{:S(2)}, u32[]{:S(2)}) async-start(f32[32,256,16]{1,2,0:T(8,128)} %stack.2), calls=%async_computation | async-start | bytes 1048576 | tf_op jit(solution)/shard_map/all_to_all | solution.py:60
  22.3 39.4 %all_gather.10 = bf16[8192,32]{0,1:T(8,128)(2,1)S(1)} all-gather(bf16[256,32]{0,1:T(8,128)(2,1)S(1)} %multiply_convert_fusion), channel_id=1, replica_groups=mesh['row'=32,'col'=8] {'row'}, dimensions={0}, use_global_device_ids=true | all-gather | bytes 540672 | tf_op jit(solution)/shard_map/all_gather | solution.py:30
  63.5 22.6 %all_gather.9 = f32[2048,16]{0,1:T(8,128)S(1)} all-gather(f32[256,16]{0,1:T(8,128)S(1)} %broadcast_multiply_fusion), channel_id=1, replica_groups=mesh['row'=32,'col'=8] {'col'}, dimensions={0}, use_global_device_ids=true | all-gather | bytes 147456 | tf_op jit(solution)/shard_map/all_gather | solution.py:57
  87.0 107.7 %while.22 = (s32[]{:T(128)}, f32[2048,32]{0,1:T(8,128)S(1)}, f32[]{:T(128)}, f32[2048]{0:T(1024)S(1)}, f32[16,512]{1,0:T(8,128)S(1)}, /*index=5*/f32[16,512,16]{...) while((s32[]{:T(128)}, f32[2048,32]{0,1:T(8,128)S(1)}, ...), condition=%wide.region_5.6_spmd.clone, body=%wide.region_4.5_spmd.clone.sunk | while | flops 274857984 | bytes 5028475 | solution.py:40
  87.0 5.3 fusion.45
  100.5 5.3 fusion.45
  107.2 5.3 fusion.45
  120.7 5.3 fusion.45
  127.4 5.3 fusion.45
  140.9 5.3 fusion.45
  147.6 5.3 fusion.45
  188.0 5.3 fusion.45
  196.1 29.2 %reduce-scatter.3.cloned.1.call-done = f32[256,32]{0,1:T(8,128)} async-done(((f32[2048,32]{0,1:T(8,128)}), f32[256,32]{0,1:T(8,128)}) %reduce-scatter.3.cloned.1.call-update) | async-done | bytes 32784 | tf_op jit(solution)/shard_map/reduce_scatter | solution.py:74
  226.2 78.3 %all-reduce = (f32[32]{0:T(128)S(1)}, f32[32]{0:T(128)S(1)}) all-reduce(f32[32]{0:T(128)S(1)} %get-tuple-element.191, f32[32]{0:T(128)S(1)} %get-tuple-element.190), channel_id=1, replica_groups=mesh['row'=32,'col'=8] {'row','col'}, use_global_device_ids=true, to_apply=%region_1.0 | all-reduce | flops 64 | bytes 512 | tf_op jit(solution)/shard_map/psum | solution.py:23
  305.4 73.1 %psum.30 = f32[32]{0:T(128)S(1)} all-reduce(f32[32]{0:T(128)S(1)} %get-tuple-element.226), channel_id=1, replica_groups=mesh['row'=32,'col'=8] {'row','col'}, use_global_device_ids=true, to_apply=%region_10.11 | all-reduce | flops 32 | bytes 256 | tf_op jit(solution)/shard_map/psum | solution.py:23
  378.6 33.5 %all_gather.11 = bf16[8192,32]{0,1:T(8,128)(2,1)S(1)} all-gather(bf16[256,32]{0,1:T(8,128)(2,1)S(1)} %fusion.26), channel_id=1, replica_groups=mesh['row'=32,'col'=8] {'row'}, dimensions={0}, use_global_device_ids=true | all-gather | bytes 540672 | tf_op jit(solution)/shard_map/all_gather | solution.py:30
  413.9 107.7 %while.23 = (s32[]{:T(128)}, f32[2048,32]{0,1:T(8,128)S(1)}, f32[]{:T(128)}, f32[2048]{0:T(1024)S(1)}, f32[16,512]{1,0:T(8,128)S(1)}, /*index=5*/f32[16,512,16]{...) while((s32[]{:T(128)}, f32[2048,32]{0,1:T(8,128)S(1)}, ...), condition=%wide.region_12.13_spmd.clone, body=%wide.region_11.12_spmd.clone.sunk | while | flops 274857984 | bytes 5028475 | solution.py:40
  434.1 5.3 fusion.50
  440.8 5.3 fusion.50
  447.6 5.3 fusion.50
  454.3 5.3 fusion.50
  461.0 5.3 fusion.50
  467.8 5.3 fusion.50
  474.5 5.3 fusion.50
  481.2 5.3 fusion.50
  488.0 5.3 fusion.50
  494.7 5.3 fusion.50
  501.5 5.3 fusion.50
  508.2 5.3 fusion.50
  514.9 5.3 fusion.50
  522.4 37.1 %reduce-scatter.5.cloned.1.call-done = f32[256,32]{0,1:T(8,128)} async-done(((f32[2048,32]{0,1:T(8,128)}), f32[256,32]{0,1:T(8,128)}) %reduce-scatter.5.cloned.1.call-update) | async-done | bytes 32784 | tf_op jit(solution)/shard_map/reduce_scatter | solution.py:74
  560.3 78.2 %psum.31 = f32[32]{0:T(128)S(1)} all-reduce(f32[32]{0:T(128)S(1)} %fusion.21), channel_id=1, replica_groups=mesh['row'=32,'col'=8] {'row','col'}, use_global_device_ids=true, to_apply=%region_15.16 | all-reduce | flops 32 | bytes 256 | tf_op jit(solution)/shard_map/psum | solution.py:76
  (108 shorter events, 116.0 us)
Async XLA Ops:
  8.8 77.3 %all-to-all-start = ((f32[32,256,16]{1,2,0:T(8,128)}), f32[32,256,16]{1,2,0:T(8,128)S(1)}, u32[]{:S(2)}, u32[]{:S(2)}) async-start(f32[32,256,16]{1,2,0:T(8,128)} %stack.2), calls=%async_computation | async-start | bytes 1048576 | tf_op jit(solution)/shard_map/all_to_all | solution.py:60
  20.8 204.5 %reduce-scatter.3.cloned.1.call-start = ((), (), s32[]{:S(2)}) async-start(), calls=%async_computation.3 | async-start | bytes 294912 | tf_op jit(solution)/shard_map/reduce_scatter | solution.py:74
  87.0 138.3 %copy-start.2 = (f32[256,32]{0,1:T(8,128)S(1)}, f32[256,32]{0,1:T(8,128)}, u32[]{:S(2)}) copy-start(f32[256,32]{0,1:T(8,128)} %param.14) | copy-start | bytes 98308
  194.7 0.7 copy-start.1
  195.4 364.0 %reduce-scatter.5.cloned.1.call-start = ((), (), s32[]{:S(2)}) async-start(), calls=%async_computation.4 | async-start | bytes 294912 | tf_op jit(solution)/shard_map/reduce_scatter | solution.py:74
  521.6 0.7 copy-start
Sparse Core Ops, SparseCore 0:
  195.5 29.7 reduce-scatter.2
  522.5 36.8 reduce-scatter.4
